TPU v7x, 128 devices: a whole 4x4x4 slice. The times are simulated.
128 devices in a mesh: frm: 8 (over z, core), vox: 16 (over y, x).
Axes of the slice: x: 4, y: 4, z: 4, core: 2. Of those that a mesh axis runs over, the one named last changes fastest.
Arguments:
- movie_matrix: bfloat16 [16384, 32768], P('frm', 'vox'), may hold values from -8 to 8
- voxel_probe: bfloat16 [32768, 64], P('vox'), may hold values from -0.03125 to 0.03125
- frame_probe: bfloat16 [16384, 64], P('frm'), may hold values from -0.046875 to 0.046875
Outputs:
- lowrank: bfloat16 [16384, 32768], P('frm', 'vox')
- sparse: bfloat16 [16384, 32768], P('frm', 'vox')
All inputs are finite; a program needn't handle non-finite values.
Results may differ from a plain program's by a relative error of at most 0.04.
Values may be sent and summed in bfloat16 or wider, within the bound.
A program may use at most 128 MiB of HBM per device.

v0:
```python
import jax
import jax.numpy as jnp
from jax import lax
from jax.sharding import Mesh
from jax.sharding import PartitionSpec as P

ITERS = 2
VOX = ("vox_0", "vox_1")
FRM = ("frm_0", "frm_1")


cutoff = 1.0
ridge_scale = 0.1


def in_blocks(x, dim, size):
    before, after = (x.shape[:dim], x.shape[dim + 1 :])
    return jnp.moveaxis(x.reshape(*before, size, -1, *after), dim, 0)


def sum_at_owner(x, axis, dim):
    tiles = in_blocks(x, dim, lax.axis_size(axis))
    arrived = lax.all_to_all(tiles, axis, split_axis=0, concat_axis=0, tiled=True)
    return arrived.sum(axis=0)


def sent_and_summed(x, axis, dim):
    size = lax.axis_size(axis)
    tiles = lax.all_to_all(in_blocks(x, dim, size), axis, 0, 0, tiled=True)
    return jnp.sum(tiles.astype(jnp.float32), axis=0)


def copy_for_each(x, axis):
    copies = jnp.broadcast_to(x, (lax.axis_size(axis), *x.shape))
    return lax.all_to_all(copies, axis, split_axis=0, concat_axis=0, tiled=True)


def over_copies(x, axis):
    everything = copy_for_each(x, axis)
    return jnp.sum(everything, axis=0)


def by_axis(x, axes):
    far, near = axes
    nearer = over_copies(x, near)
    return over_copies(nearer, far)


def joined_along(tiles, dim):
    shape = list(tiles.shape[1:])
    shape[dim] *= tiles.shape[0]
    return jnp.moveaxis(tiles, 0, dim).reshape(shape)


def gathered_copies(x, axis, dim):
    return joined_along(copy_for_each(x, axis), dim)


def core_map(core_matrix):
    gram_matrix = jnp.dot(
        core_matrix.T,
        core_matrix,
        precision=lax.Precision.HIGHEST,
        preferred_element_type=jnp.float32,
    )
    core_order = core_matrix.shape[0]
    ridge_shift = ridge_scale * (jnp.trace(gram_matrix) / core_order + 1e-06)
    factor = jnp.linalg.cholesky(gram_matrix + ridge_shift * jnp.eye(core_order, dtype=jnp.float32))
    return jax.scipy.linalg.cho_solve((factor, True), core_matrix.T)


def shrink(values):
    return jnp.sign(values) * jnp.maximum(jnp.abs(values) - cutoff, 0.0)


def project_core(probe_rows, sketch_rows):
    return lax.dot_general(
        probe_rows,
        sketch_rows,
        (((0,), (0,)), ((), ())),
        precision=lax.Precision.HIGHEST,
        preferred_element_type=jnp.float32,
    )


def on_device(movie_matrix, voxel_probe, frame_probe):
    frame_count = movie_matrix.shape[0]
    vox_count = lax.axis_size(VOX)
    vox_index = lax.axis_index(VOX)
    frame_share = frame_count // vox_count
    probe_wide = frame_probe.astype(jnp.float32)
    sparse = jnp.zeros_like(movie_matrix)
    lowrank = jnp.zeros(movie_matrix.shape, jnp.float32)
    for iteration in range(ITERS):
        current = (movie_matrix.astype(jnp.float32) - sparse.astype(jnp.float32)).astype(
            jnp.bfloat16
        )
        frame_part = jnp.dot(current, voxel_probe, preferred_element_type=jnp.float32)
        voxel_part = lax.dot_general(
            current, frame_probe, (((0,), (0,)), ((), ())), preferred_element_type=jnp.float32
        )
        probe_rows = lax.dynamic_slice_in_dim(probe_wide, vox_index * frame_share, frame_share, 0)
        own_frames = sum_at_owner(frame_part, VOX, 0)
        voxel_rows = sent_and_summed(voxel_part.astype(jnp.bfloat16), FRM, 0)
        core_matrix = by_axis(
            project_core(probe_rows, own_frames), (("frm_0", "frm_1"), ("vox_0", "vox_1"))
        )
        core_mixer = core_map(core_matrix)
        left_rows = jnp.dot(
            own_frames,
            core_mixer,
            precision=lax.Precision.HIGHEST,
            preferred_element_type=jnp.float32,
        ).astype(jnp.bfloat16)
        left_factor = gathered_copies(left_rows, VOX, 0)
        right_factor = gathered_copies(voxel_rows.astype(jnp.bfloat16), FRM, 0)
        lowrank = lax.dot_general(
            left_factor, right_factor, (((1,), (1,)), ((), ())), preferred_element_type=jnp.float32
        )
        sparse = shrink(movie_matrix.astype(jnp.float32) - lowrank).astype(jnp.bfloat16)
    return (lowrank.astype(jnp.bfloat16), sparse)


def solution(mesh):
    finer = Mesh(mesh.devices.reshape(4, 2, 4, 4), ("frm_0", "frm_1", "vox_0", "vox_1"))
    return jax.shard_map(
        on_device,
        mesh=finer,
        in_specs=(P(FRM, VOX), P(VOX, None), P(FRM, None)),
        out_specs=(P(FRM, VOX), P(FRM, VOX)),
        check_vma=False,
    )
```

profile of v0, /device:TPU:0, one launch (start us, length us, event | category | flops | bytes accessed | tf_op | source)
XLA Modules:
  0.0 209.3 jit_solution(5791175311153524397)
XLA Ops:
  0.6 6.1 %convolution_bitcast_fusion.1 = f32[8,16,8,128]{3,2,1,0:T(8,128)S(1)} fusion(bf16[2048,2048]{1,0:T(8,128)(2,1)} %param.6, bf16[2048,64]{0,1:T(8,128)(2,1)} %param.7), kind=kOutput, calls=%fused_computation.9 | convolution fusion | flops 536870912 | bytes 9175040 | tf_op jit(solution)/shard_map/dot_general | solution.py:98
  6.7 0.9 copy.92
  7.6 7.1 %all-to-all-start = ((f32[16,128,64]{1,2,0:T(8,128)}), f32[16,128,64]{1,2,0:T(8,128)S(1)}, u32[]{:S(2)}, u32[]{:S(2)}) async-start(f32[16,128,64]{1,2,0:T(8,128)} %bitcast.85), calls=%async_computation | async-start | bytes 1048576 | tf_op jit(solution)/shard_map/all_to_all | solution.py:23
  14.7 11.5 %all-to-all-done = f32[16,128,64]{1,2,0:T(8,128)S(1)} async-done(((f32[16,128,64]{1,2,0:T(8,128)}), f32[16,128,64]{1,2,0:T(8,128)S(1)}, u32[]{:S(2)}, u32[]{:S(2)}) %all-to-all-start) | async-done | bytes 524320 | tf_op jit(solution)/shard_map/all_to_all | solution.py:23
  26.5 1.0 reshape.46
  27.5 3.5 %all-to-all-start.1 = ((f32[16,1,4096]{2,1,0:T(1,128)}), f32[16,1,4096]{2,1,0:T(1,128)S(1)}, u32[]{:S(2)}, u32[]{:S(2)}) async-start(f32[16,1,4096]{2,1,0:T(1,128)} %reshape.46), calls=%async_computation.1 | async-start | bytes 524288 | tf_op jit(solution)/shard_map/all_to_all | solution.py:35
  31.1 5.0 %convolution_convert_fusion.1 = bf16[2048,64]{0,1:T(8,128)(2,1)S(1)} fusion(bf16[2048,64]{0,1:T(8,128)(2,1)S(1)} %copy-done, bf16[2048,2048]{1,0:T(8,128)(2,1)} %param.6), kind=kOutput, calls=%fused_computation.7 | convolution fusion | flops 537001984 | bytes 8912896 | tf_op jit(solution)/shard_map/dot_general | solution.py:99
  36.0 0.7 copy.94
  36.8 3.0 %all-to-all-done.1 = f32[16,1,4096]{2,1,0:T(1,128)S(1)} async-done(((f32[16,1,4096]{2,1,0:T(1,128)}), f32[16,1,4096]{2,1,0:T(1,128)S(1)}, u32[]{:S(2)}, u32[]{:S(2)}) %all-to-all-start.1) | async-done | bytes 262176 | tf_op jit(solution)/shard_map/all_to_all | solution.py:35
  39.7 5.3 %all-to-all-start.4 = ((bf16[8,256,64]{1,2,0:T(8,128)(2,1)}), bf16[8,256,64]{1,2,0:T(8,128)(2,1)S(1)}, u32[]{:S(2)}, u32[]{:S(2)}) async-start(bf16[8,256,64]{1,2,0:T(8,128)(2,1)} %bitcast.87), calls=%async_computation.4 | async-start | bytes 524288 | tf_op jit(solution)/shard_map/all_to_all | solution.py:29
  45.6 1.3 reduce.6
  47.2 0.8 reshape.48
  48.1 4.5 %all-to-all-done.4 = bf16[8,256,64]{1,2,0:T(8,128)(2,1)S(1)} async-done(((bf16[8,256,64]{1,2,0:T(8,128)(2,1)}), bf16[8,256,64]{1,2,0:T(8,128)(2,1)S(1)}, u32[]{:S(2)}, u32[]{:S(2)}) %all-to-all-start.4) | async-done | bytes 262176 | tf_op jit(solution)/shard_map/all_to_all | solution.py:29
  52.6 3.4 %all-to-all-start.2 = ((f32[8,1,4096]{2,1,0:T(1,128)}), f32[8,1,4096]{2,1,0:T(1,128)S(1)}, u32[]{:S(2)}, u32[]{:S(2)}) async-start(f32[8,1,4096]{2,1,0:T(1,128)} %reshape.48), calls=%async_computation.2 | async-start | bytes 262144 | tf_op jit(solution)/shard_map/all_to_all | solution.py:35
  56.0 6.0 %all-to-all-done.2 = f32[8,1,4096]{2,1,0:T(1,128)S(1)} async-done(((f32[8,1,4096]{2,1,0:T(1,128)}), f32[8,1,4096]{2,1,0:T(1,128)S(1)}, u32[]{:S(2)}, u32[]{:S(2)}) %all-to-all-start.2) | async-done | bytes 131104 | tf_op jit(solution)/shard_map/all_to_all | solution.py:35
  62.0 0.7 broadcast_in_dim.37
  62.7 3.4 %all-to-all-start.5 = ((bf16[8,256,64]{1,2,0:T(8,128)(2,1)}), bf16[8,256,64]{1,2,0:T(8,128)(2,1)S(1)}, u32[]{:S(2)}, u32[]{:S(2)}) async-start(bf16[8,256,64]{1,2,0:T(8,128)(2,1)} %broadcast_in_dim.37), calls=%async_computation.5 | async-start | bytes 524288 | tf_op jit(solution)/shard_map/all_to_all | solution.py:35
  66.2 1.0 reduce.7
  67.3 0.8 select_reduce_fusion.3
  68.9 5.8 %cholesky.44 = f32[64,64]{1,0:T(8,128)S(1)} custom-call(f32[64,64]{1,0:T(8,128)S(1)} %fusion.19), custom_call_target="Cholesky" | custom-call | tf_op jit(solution)/shard_map/jit(cholesky)/cholesky | solution.py:68
  76.1 4.9 %custom-call.8 = f32[1,64,64]{1,2,0:T(8,128)S(1)} custom-call(f32[1,64,64]{2,1,0:T(8,128)S(1)} %fusion.6), custom_call_target="InvertDiagBlocksLowerTriangular" | custom-call | tf_op jit(solution)/shard_map/jit(_cho_solve)/triangular_solve | solution.py:69
  81.7 0.8 broadcast_in_dim.36
  82.4 4.2 %all-to-all-start.3 = ((bf16[16,128,64]{1,2,0:T(8,128)(2,1)}), bf16[16,128,64]{1,2,0:T(8,128)(2,1)S(1)}, u32[]{:S(2)}, u32[]{:S(2)}) async-start(bf16[16,128,64]{1,2,0:T(8,128)(2,1)} %broadcast_in_dim.36), calls=%async_computation.3 | async-start | bytes 524288 | tf_op jit(solution)/shard_map/all_to_all | solution.py:35
  86.7 9.2 %all-to-all-done.3 = bf16[16,128,64]{1,2,0:T(8,128)(2,1)S(1)} async-done(((bf16[16,128,64]{1,2,0:T(8,128)(2,1)}), bf16[16,128,64]{1,2,0:T(8,128)(2,1)S(1)}, u32[]{:S(2)}, u32[]{:S(2)}) %all-to-all-start.3) | async-done | bytes 262176 | tf_op jit(solution)/shard_map/all_to_all | solution.py:35
  95.9 11.1 %fusion = bf16[2048,2048]{1,0:T(8,128)(2,1)S(1)} fusion(bf16[2048,2048]{1,0:T(8,128)(2,1)} %param.6, bf16[2048,64]{0,1:T(8,128)(2,1)S(1)} %bitcast.94, bf16[16,128,64]{1,2,0:T(8,128)(2,1)S(1)} %all-to-all-done.3), kind=kOutput, calls=%fused_computation.3 | convolution fusion | flops 583008256 | bytes 17301504 | tf_op jit(solution)/shard_map/dot_general | solution.py:117
  107.0 3.4 %copy-done.1 = bf16[2048,2048]{1,0:T(8,128)(2,1)} copy-done((bf16[2048,2048]{1,0:T(8,128)(2,1)}, bf16[2048,2048]{1,0:T(8,128)(2,1)S(1)}, u32[]{:S(2)}) %copy-start.1) | copy-done | bytes 8388632
  110.4 2.6 %convolution_bitcast_fusion = f32[8,16,8,128]{3,2,1,0:T(8,128)S(1)} fusion(bf16[2048,2048]{1,0:T(8,128)(2,1)S(1)} %fusion, bf16[2048,64]{0,1:T(8,128)(2,1)S(1)} %copy-done.2), kind=kOutput, calls=%fused_computation.8 | convolution fusion | flops 536870912 | bytes 9175040 | tf_op jit(solution)/shard_map/dot_general | solution.py:98
  113.1 13.9 %all_to_all.60 = f32[16,128,64]{1,2,0:T(8,128)S(1)} all-to-all(f32[16,128,64]{1,2,0:T(8,128)S(1)} %bitcast.88), channel_id=1, replica_groups=mesh['frm_0'=4,'frm_1'=2,'vox_0'=4,'vox_1'=4] {'vox_0','vox_1'}, dimensions={0} | all-to-all | bytes 1048576 | tf_op jit(solution)/shard_map/all_to_all | solution.py:23
  127.3 1.0 reshape.50
  128.3 3.5 %all-to-all-start.7 = ((f32[16,1,4096]{2,1,0:T(1,128)}), f32[16,1,4096]{2,1,0:T(1,128)S(1)}, u32[]{:S(2)}, u32[]{:S(2)}) async-start(f32[16,1,4096]{2,1,0:T(1,128)} %reshape.50), calls=%async_computation.7 | async-start | bytes 524288 | tf_op jit(solution)/shard_map/all_to_all | solution.py:35
  131.9 5.0 %convolution_convert_fusion = bf16[2048,64]{0,1:T(8,128)(2,1)S(1)} fusion(bf16[2048,64]{0,1:T(8,128)(2,1)S(1)} %copy-done, bf16[2048,2048]{1,0:T(8,128)(2,1)} %copy-done.1), kind=kOutput, calls=%fused_computation.6 | convolution fusion | flops 537001984 | bytes 8912896 | tf_op jit(solution)/shard_map/dot_general | solution.py:99
  136.8 0.7 copy.93
  137.5 3.0 %all-to-all-done.7 = f32[16,1,4096]{2,1,0:T(1,128)S(1)} async-done(((f32[16,1,4096]{2,1,0:T(1,128)}), f32[16,1,4096]{2,1,0:T(1,128)S(1)}, u32[]{:S(2)}, u32[]{:S(2)}) %all-to-all-start.7) | async-done | bytes 262176 | tf_op jit(solution)/shard_map/all_to_all | solution.py:35
  140.5 4.2 %all-to-all-start.10 = ((bf16[8,256,64]{1,2,0:T(8,128)(2,1)}), bf16[8,256,64]{1,2,0:T(8,128)(2,1)S(1)}, u32[]{:S(2)}, u32[]{:S(2)}) async-start(bf16[8,256,64]{1,2,0:T(8,128)(2,1)} %bitcast.86), calls=%async_computation.10 | async-start | bytes 524288 | tf_op jit(solution)/shard_map/all_to_all | solution.py:29
  144.8 1.3 reduce.8
  146.4 0.8 reshape.52
  147.2 5.1 %all-to-all-done.10 = bf16[8,256,64]{1,2,0:T(8,128)(2,1)S(1)} async-done(((bf16[8,256,64]{1,2,0:T(8,128)(2,1)}), bf16[8,256,64]{1,2,0:T(8,128)(2,1)S(1)}, u32[]{:S(2)}, u32[]{:S(2)}) %all-to-all-start.10) | async-done | bytes 262176 | tf_op jit(solution)/shard_map/all_to_all | solution.py:29
  152.3 3.4 %all-to-all-start.8 = ((f32[8,1,4096]{2,1,0:T(1,128)}), f32[8,1,4096]{2,1,0:T(1,128)S(1)}, u32[]{:S(2)}, u32[]{:S(2)}) async-start(f32[8,1,4096]{2,1,0:T(1,128)} %reshape.52), calls=%async_computation.8 | async-start | bytes 262144 | tf_op jit(solution)/shard_map/all_to_all | solution.py:35
  155.7 6.0 %all-to-all-done.8 = f32[8,1,4096]{2,1,0:T(1,128)S(1)} async-done(((f32[8,1,4096]{2,1,0:T(1,128)}), f32[8,1,4096]{2,1,0:T(1,128)S(1)}, u32[]{:S(2)}, u32[]{:S(2)}) %all-to-all-start.8) | async-done | bytes 131104 | tf_op jit(solution)/shard_map/all_to_all | solution.py:35
  162.5 3.6 %all-to-all-start.11 = ((bf16[8,256,64]{1,2,0:T(8,128)(2,1)}), bf16[8,256,64]{1,2,0:T(8,128)(2,1)S(1)}, u32[]{:S(2)}, u32[]{:S(2)}) async-start(bf16[8,256,64]{1,2,0:T(8,128)(2,1)} %broadcast_in_dim.42), calls=%async_computation.11 | async-start | bytes 524288 | tf_op jit(solution)/shard_map/all_to_all | solution.py:35
  166.1 1.0 reduce.9
  167.2 0.8 select_reduce_fusion.2
  168.8 5.8 %cholesky.55 = f32[64,64]{1,0:T(8,128)S(1)} custom-call(f32[64,64]{1,0:T(8,128)S(1)} %fusion.13), custom_call_target="Cholesky" | custom-call | tf_op jit(solution)/shard_map/jit(cholesky)/cholesky | solution.py:68
  176.0 4.9 %custom-call.9 = f32[1,64,64]{1,2,0:T(8,128)S(1)} custom-call(f32[1,64,64]{2,1,0:T(8,128)S(1)} %fusion.7), custom_call_target="InvertDiagBlocksLowerTriangular" | custom-call | tf_op jit(solution)/shard_map/jit(_cho_solve)/triangular_solve | solution.py:69
  181.6 0.8 broadcast_in_dim.41
  182.4 4.2 %all-to-all-start.9 = ((bf16[16,128,64]{1,2,0:T(8,128)(2,1)}), bf16[16,128,64]{1,2,0:T(8,128)(2,1)S(1)}, u32[]{:S(2)}, u32[]{:S(2)}) async-start(bf16[16,128,64]{1,2,0:T(8,128)(2,1)} %broadcast_in_dim.41), calls=%async_computation.9 | async-start | bytes 524288 | tf_op jit(solution)/shard_map/all_to_all | solution.py:35
  186.6 9.0 %all-to-all-done.9 = bf16[16,128,64]{1,2,0:T(8,128)(2,1)S(1)} async-done(((bf16[16,128,64]{1,2,0:T(8,128)(2,1)}), bf16[16,128,64]{1,2,0:T(8,128)(2,1)S(1)}, u32[]{:S(2)}, u32[]{:S(2)}) %all-to-all-start.9) | async-done | bytes 262176 | tf_op jit(solution)/shard_map/all_to_all | solution.py:35
  195.6 13.7 %multiply_convert_fusion = (bf16[2048,2048]{1,0:T(8,128)(2,1)}, bf16[2048,2048]{1,0:T(8,128)(2,1)}) fusion(bf16[2048,2048]{1,0:T(8,128)(2,1)} %param.6, bf16[2048,64]{0,1:T(8,128)(2,1)S(1)} %bitcast.93, bf16[16,128,64]{1,2,0:T(8,128)(2,1)S(1)} %all-to-all-done.9), kind=kOutput, calls=%fused_computation.4 | convolution fusion | flops 574619648 | bytes 25690112 | tf_op jit(solution)/shard_map/dot_general | solution.py:117
  (48 shorter events, 7.0 us)
Async XLA Ops:
  0.6 25.6 %copy-start = (bf16[2048,64]{0,1:T(8,128)(2,1)S(1)}, bf16[2048,64]{0,1:T(8,128)(2,1)}, u32[]{:S(2)}) copy-start(bf16[2048,64]{0,1:T(8,128)(2,1)} %param.8) | copy-start | bytes 786436
  7.6 18.7 %all-to-all-start = ((f32[16,128,64]{1,2,0:T(8,128)}), f32[16,128,64]{1,2,0:T(8,128)S(1)}, u32[]{:S(2)}, u32[]{:S(2)}) async-start(f32[16,128,64]{1,2,0:T(8,128)} %bitcast.85), calls=%async_computation | async-start | bytes 1048576 | tf_op jit(solution)/shard_map/all_to_all | solution.py:23
  27.5 12.2 %all-to-all-start.1 = ((f32[16,1,4096]{2,1,0:T(1,128)}), f32[16,1,4096]{2,1,0:T(1,128)S(1)}, u32[]{:S(2)}, u32[]{:S(2)}) async-start(f32[16,1,4096]{2,1,0:T(1,128)} %reshape.46), calls=%async_computation.1 | async-start | bytes 524288 | tf_op jit(solution)/shard_map/all_to_all | solution.py:35
  39.7 12.9 %all-to-all-start.4 = ((bf16[8,256,64]{1,2,0:T(8,128)(2,1)}), bf16[8,256,64]{1,2,0:T(8,128)(2,1)S(1)}, u32[]{:S(2)}, u32[]{:S(2)}) async-start(bf16[8,256,64]{1,2,0:T(8,128)(2,1)} %bitcast.87), calls=%async_computation.4 | async-start | bytes 524288 | tf_op jit(solution)/shard_map/all_to_all | solution.py:29
  52.6 9.4 %all-to-all-start.2 = ((f32[8,1,4096]{2,1,0:T(1,128)}), f32[8,1,4096]{2,1,0:T(1,128)S(1)}, u32[]{:S(2)}, u32[]{:S(2)}) async-start(f32[8,1,4096]{2,1,0:T(1,128)} %reshape.48), calls=%async_computation.2 | async-start | bytes 262144 | tf_op jit(solution)/shard_map/all_to_all | solution.py:35
  62.7 18.9 %all-to-all-start.5 = ((bf16[8,256,64]{1,2,0:T(8,128)(2,1)}), bf16[8,256,64]{1,2,0:T(8,128)(2,1)S(1)}, u32[]{:S(2)}, u32[]{:S(2)}) async-start(bf16[8,256,64]{1,2,0:T(8,128)(2,1)} %broadcast_in_dim.37), calls=%async_computation.5 | async-start | bytes 524288 | tf_op jit(solution)/shard_map/all_to_all | solution.py:35
  82.4 13.5 %all-to-all-start.3 = ((bf16[16,128,64]{1,2,0:T(8,128)(2,1)}), bf16[16,128,64]{1,2,0:T(8,128)(2,1)S(1)}, u32[]{:S(2)}, u32[]{:S(2)}) async-start(bf16[16,128,64]{1,2,0:T(8,128)(2,1)} %broadcast_in_dim.36), calls=%async_computation.3 | async-start | bytes 524288 | tf_op jit(solution)/shard_map/all_to_all | solution.py:35
  95.9 14.5 %copy-start.2 = (bf16[2048,64]{0,1:T(8,128)(2,1)S(1)}, bf16[2048,64]{0,1:T(8,128)(2,1)}, u32[]{:S(2)}) copy-start(bf16[2048,64]{0,1:T(8,128)(2,1)} %param.7) | copy-start | bytes 786436
  107.0 3.4 %copy-start.1 = (bf16[2048,2048]{1,0:T(8,128)(2,1)}, bf16[2048,2048]{1,0:T(8,128)(2,1)S(1)}, u32[]{:S(2)}) copy-start(bf16[2048,2048]{1,0:T(8,128)(2,1)S(1)} %fusion) | copy-start | bytes 25165828
  128.3 12.2 %all-to-all-start.7 = ((f32[16,1,4096]{2,1,0:T(1,128)}), f32[16,1,4096]{2,1,0:T(1,128)S(1)}, u32[]{:S(2)}, u32[]{:S(2)}) async-start(f32[16,1,4096]{2,1,0:T(1,128)} %reshape.50), calls=%async_computation.7 | async-start | bytes 524288 | tf_op jit(solution)/shard_map/all_to_all | solution.py:35
  140.5 11.8 %all-to-all-start.10 = ((bf16[8,256,64]{1,2,0:T(8,128)(2,1)}), bf16[8,256,64]{1,2,0:T(8,128)(2,1)S(1)}, u32[]{:S(2)}, u32[]{:S(2)}) async-start(bf16[8,256,64]{1,2,0:T(8,128)(2,1)} %bitcast.86), calls=%async_computation.10 | async-start | bytes 524288 | tf_op jit(solution)/shard_map/all_to_all | solution.py:29
  152.3 9.4 %all-to-all-start.8 = ((f32[8,1,4096]{2,1,0:T(1,128)}), f32[8,1,4096]{2,1,0:T(1,128)S(1)}, u32[]{:S(2)}, u32[]{:S(2)}) async-start(f32[8,1,4096]{2,1,0:T(1,128)} %reshape.52), calls=%async_computation.8 | async-start | bytes 262144 | tf_op jit(solution)/shard_map/all_to_all | solution.py:35
  162.5 19.2 %all-to-all-start.11 = ((bf16[8,256,64]{1,2,0:T(8,128)(2,1)}), bf16[8,256,64]{1,2,0:T(8,128)(2,1)S(1)}, u32[]{:S(2)}, u32[]{:S(2)}) async-start(bf16[8,256,64]{1,2,0:T(8,128)(2,1)} %broadcast_in_dim.42), calls=%async_computation.11 | async-start | bytes 524288 | tf_op jit(solution)/shard_map/all_to_all | solution.py:35
  182.4 13.2 %all-to-all-start.9 = ((bf16[16,128,64]{1,2,0:T(8,128)(2,1)}), bf16[16,128,64]{1,2,0:T(8,128)(2,1)S(1)}, u32[]{:S(2)}, u32[]{:S(2)}) async-start(bf16[16,128,64]{1,2,0:T(8,128)(2,1)} %broadcast_in_dim.41), calls=%async_computation.9 | async-start | bytes 524288 | tf_op jit(solution)/shard_map/all_to_all | solution.py:35
where the time goes:
time: 211 us; the launch traced here: 209 us
  waiting for transfers between devices  57.3 us (27%)
  matrix products  46.7 us (22%)
  starting transfers between devices  45.9 us (22%)
  other arithmetic  29.1 us (14%)
  local copies, waits for them, and re-layouts  14 us (7%)
  blocking collectives  13.9 us (7%)
  between operations  2.36 us (1%)
    all_to_all x8, waiting for transfers between devices, copy_for_each(): return lax.all_to_all(copies, axis, split_axis=0, concat_axis=0, tiled=True)  36.2 us
    all_to_all x8, starting transfers between devices, copy_for_each(): return lax.all_to_all(copies, axis, split_axis=0, concat_axis=0, tiled=True)  29.2 us
    dot_general x2, matrix products, on_device(): lax.dot_general(left_factor, right_factor, (((1,), (1,)), ((), ())), pref...  24.8 us
    all_to_all x1, blocking collectives, sum_at_owner(): lax.all_to_all(tiles, axis, split_axis=0, concat_axis=0, tiled=True)  13.9 us
    another operation x6, other arithmetic, core_map(): jnp.linalg.cholesky(gram_matrix + ridge_shift * jnp.eye(core_order, dtype...  13 us
    all_to_all x1, waiting for transfers between devices, sum_at_owner(): lax.all_to_all(tiles, axis, split_axis=0, concat_axis=0, tiled=True)  11.5 us
    another operation x4, other arithmetic, core_map(): return jax.scipy.linalg.cho_solve((factor, True), core_matrix.T)  11.1 us
    dot_general x2, matrix products, on_device(): lax.dot_general(current, frame_probe, (((0,), (0,)), ((), ())), preferred...  9.9 us
  transfers between devices with their start and end apart: 11, of which 9 were waited for; matrix products, arithmetic and copies ran while one was open for 22% of the time, Pallas kernels for 0%

commit v1 on v0

v1 whole, which is shorter than its diff:
```python
import functools

import jax
import jax.numpy as jnp
from jax import lax
from jax.experimental import pallas as pl
from jax.experimental.pallas import tpu as pltpu
from jax.sharding import PartitionSpec as P

MESH = pl.DeviceIdType.MESH
BF16, F32 = jnp.bfloat16, jnp.float32
ITERS = 2
RANK = 64
LANES = 128
cutoff = 1.0
ridge_scale = 0.1
NN = (((1,), (0,)), ((), ()))
NT = (((1,), (1,)), ((), ()))
TN = (((0,), (0,)), ((), ()))


def mm(a, b, dims):
    return lax.dot_general(a, b, dims, preferred_element_type=F32)


def split(x):
    high = x.astype(BF16)
    return high, (x - high.astype(F32)).astype(BF16)


def solve(blocks):
    row_id = lax.broadcasted_iota(jnp.int32, (8, LANES), 0)

    def step(_, blocks):
        panel = blocks[0]
        for k in range(8):
            column, row = panel[:, k : k + 1], panel[k : k + 1, :]
            row = row / panel[k : k + 1, k : k + 1]
            panel = jnp.where(row_id == k, row, panel - column * row)
        others = []
        for block in blocks[1:]:
            for k in range(8):
                block = block - blocks_column(block, k) * panel[k : k + 1, :]
            others.append(pltpu.roll(block, LANES - 8, 1))
        return (*others, pltpu.roll(panel, LANES - 8, 1))

    def blocks_column(block, k):
        return block[:, k : k + 1]

    return lax.fori_loop(0, len(blocks), step, tuple(blocks))


def square(t):
    first, rest = t.astype(BF16), t - t.astype(BF16).astype(F32)
    second, third = rest.astype(BF16), (rest - rest.astype(BF16).astype(F32)).astype(BF16)
    tall = [jnp.concatenate([x, jnp.zeros_like(x)], axis=0) for x in (first, second, third)]
    small = mm(first, tall[2], NT) + mm(third, tall[0], NT) + mm(second, tall[1], NT)
    return small + (mm(first, tall[1], NT) + mm(second, tall[0], NT)) + mm(first, tall[0], NT)


def mixer_of(t):
    order = RANK
    gram = square(t)
    shift = ridge_scale * (jnp.sum(t * t) / order + 1e-06)
    rows = lax.broadcasted_iota(jnp.int32, t.shape, 0)
    lanes = lax.broadcasted_iota(jnp.int32, t.shape, 1)
    wide = gram + t + jnp.where(rows == lanes, shift, 0.0)
    blocks = solve([wide[8 * b : 8 * b + 8] for b in range(order // 8)])
    return jnp.concatenate(blocks, axis=0)[:, :order]


def sketch_kernel(
    nv, nf,
    m_hbm, vpt, fpt, ft_out, w_out,
    m_buf, f_send, f_recv, ft_full, v_send, v_recv, vt_full, t_acc, t_send, t_recv, t_sum, t_wide, t_full, w_buf, mix,
    m_sem, f_sem, fg_sem, v_sem, vg_sem, ta_sem, tb_sem, tc_sem,
):
    mv, mf = lax.axis_index("vox"), lax.axis_index("frm")
    frames, voxels = m_buf.shape
    fb, vb = frames // nv, voxels // nf
    rows = 2 * fb
    chunks = nv // 2

    def chunk_of(s):
        return lax.rem(mv // 2 + 1 + s, chunks)

    def rows_of(c):
        return pl.ds(pl.multiple_of(c * rows, rows), rows)

    def load(s):
        c = chunk_of(s)
        return pltpu.make_async_copy(m_hbm.at[rows_of(c)], m_buf.at[rows_of(c)], m_sem.at[s])

    for s in range(chunks):
        load(s).start()

    barrier = pltpu.get_barrier_semaphore()
    for d in range(1, nv):
        pl.semaphore_signal(barrier, inc=1, device_id={"vox": lax.rem(mv + d, nv)}, device_id_type=MESH)
    for d in range(1, nf):
        pl.semaphore_signal(barrier, inc=1, device_id={"frm": lax.rem(mf + d, nf)}, device_id_type=MESH)

    pl.semaphore_wait(barrier, nv + nf - 2)

    def to_vox(src, dst, sems, it, target):
        return pltpu.make_async_remote_copy(
            src_ref=src, dst_ref=dst, send_sem=sems.at[it, 0], recv_sem=sems.at[it, 1],
            device_id={"vox": target}, device_id_type=MESH,
        )

    def to_frm(src, dst, sems, it, target):
        return pltpu.make_async_remote_copy(
            src_ref=src, dst_ref=dst, send_sem=sems.at[it, 0], recv_sem=sems.at[it, 1],
            device_id={"frm": target}, device_id_type=MESH,
        )

    def all_of(ref, sems, it, axis, me, size):
        target = lax.rem(me + 1, size)
        return (to_vox if axis == "vox" else to_frm)(ref, ref, sems, it, target)

    for it in range(ITERS):
        t_acc[...] = jnp.zeros_like(t_acc)

        def frame_step(s, carry):
            c = chunk_of(s)
            if it == 0:
                load(s).wait()
            else:
                fblock = jnp.concatenate([ft_full[it - 1, 2 * c], ft_full[it - 1, 2 * c + 1]], axis=1)
                for j in range(nf):
                    cols = pl.ds(j * vb, vb)
                    low = mm(fblock, w_buf[:, cols], TN)
                    m = m_buf[rows_of(c), cols]
                    floor, roof = (low - cutoff).astype(BF16), (low + cutoff).astype(BF16)
                    m_buf[rows_of(c), cols] = jnp.minimum(jnp.maximum(m, floor), roof)
            ft = mm(vpt[...], m_buf[rows_of(c), :], NT)
            high, low_part = split(ft)
            f_send[it, 2 * c] = high[:, :fb]
            f_send[it, 2 * c + 1] = high[:, fb:]
            probe = fpt[:, rows_of(c)]
            t_acc[...] += mm(high, probe, NT) + mm(low_part, probe, NT)
            for h in range(2):
                owner = 2 * c + h

                @pl.when(owner != mv)
                def _():
                    slot = lax.rem(owner - mv + nv, nv) - 1
                    to_vox(f_send.at[it, owner], f_recv.at[it, slot], f_sem, it, owner).start()

            return carry

        lax.fori_loop(0, chunks, frame_step, 0)

        t = jnp.concatenate([jnp.zeros_like(t_acc), t_acc[...]], axis=1)
        for b in range(nf):
            t_send[it, b] = t[8 * b : 8 * b + 8]
        for d in range(1, nf):
            target = lax.rem(mf + d, nf)
            to_frm(t_send.at[it, target], t_recv.at[it, d - 1], ta_sem, it, target).start()

        def voxel_step(s, carry):
            c = lax.rem(mf + 1 + s, nf)
            cols = pl.ds(pl.multiple_of(c * vb, vb), vb)
            vt = mm(fpt[...], m_buf[:, cols], NN)
            v_send[it, c] = vt.astype(BF16)

            @pl.when(c != mf)
            def _():
                slot = lax.rem(c - mf + nf, nf) - 1
                to_frm(v_send.at[it, c], v_recv.at[it, slot], v_sem, it, c).start()

            return carry

        third = nf // 4
        lax.fori_loop(0, third, voxel_step, 0)

        all_of(t_recv.at[it], ta_sem, it, "frm", mf, nf).wait_recv()
        part = t_send[it, mf]
        for d in range(nf - 1):
            part = part + t_recv[it, d]
        t_sum[it] = part
        for d in range(1, nv):
            to_vox(t_sum.at[it], t_wide.at[it, d - 1], tb_sem, it, lax.rem(mv + d, nv)).start()

        lax.fori_loop(third, 2 * third, voxel_step, 0)

        all_of(f_recv.at[it], f_sem, it, "vox", mv, nv).wait_recv()
        share = f_send[it, mv].astype(F32)
        for d in range(nv - 1):
            share = share + f_recv[it, d].astype(F32)
        ft_full[it, mv] = share.astype(BF16)
        for d in range(1, nv):
            to_vox(ft_full.at[it, mv], ft_full.at[it, mv], fg_sem, it, lax.rem(mv + d, nv)).start()

        lax.fori_loop(2 * third, 3 * third, voxel_step, 0)

        all_of(t_wide.at[it], tb_sem, it, "vox", mv, nv).wait_recv()
        part = t_sum[it]
        for d in range(nv - 1):
            part = part + t_wide[it, d]
        t_full[it, mf] = part
        for d in range(1, nf):
            to_frm(t_full.at[it, mf], t_full.at[it, mf], tc_sem, it, lax.rem(mf + d, nf)).start()

        lax.fori_loop(3 * third, nf, voxel_step, 0)

        all_of(v_recv.at[it], v_sem, it, "frm", mf, nf).wait_recv()
        share = v_send[it, mf].astype(F32)
        for d in range(nf - 1):
            share = share + v_recv[it, d].astype(F32)
        vt_full[it, mf] = share.astype(BF16)
        for d in range(1, nf):
            to_frm(vt_full.at[it, mf], vt_full.at[it, mf], vg_sem, it, lax.rem(mf + d, nf)).start()

        all_of(t_full.at[it, pl.ds(0, nf - 1)], tc_sem, it, "frm", mf, nf).wait_recv()
        mixer = mixer_of(jnp.concatenate([t_full[it, b] for b in range(nf)], axis=0))
        mix[0], mix[1] = split(mixer)

        all_of(vt_full.at[it, pl.ds(0, nf - 1)], vg_sem, it, "frm", mf, nf).wait_recv()
        for b in range(nf):
            right = vt_full[it, b]
            w = mm(mix[0], right, NN) + mm(mix[1], right, NN)
            w_buf[:, b * vb : (b + 1) * vb] = w.astype(BF16)
        all_of(ft_full.at[it, pl.ds(0, nv - 1)], fg_sem, it, "vox", mv, nv).wait_recv()

    ft_out[...] = ft_full[ITERS - 1]
    w_out[...] = w_buf[...]
    for it in range(ITERS):
        all_of(f_recv.at[it], f_sem, it, "vox", mv, nv).wait_send()
        all_of(ft_full.at[it, pl.ds(0, nv - 1)], fg_sem, it, "vox", mv, nv).wait_send()
        all_of(v_recv.at[it], v_sem, it, "frm", mf, nf).wait_send()
        all_of(vt_full.at[it, pl.ds(0, nf - 1)], vg_sem, it, "frm", mf, nf).wait_send()
        all_of(t_recv.at[it], ta_sem, it, "frm", mf, nf).wait_send()
        all_of(t_wide.at[it], tb_sem, it, "vox", mv, nv).wait_send()
        all_of(t_full.at[it, pl.ds(0, nf - 1)], tc_sem, it, "frm", mf, nf).wait_send()


def output_kernel(m_ref, ft_ref, w_ref, low_ref, sparse_ref):
    fblock = jnp.concatenate([ft_ref[i] for i in range(ft_ref.shape[0])], axis=1)
    width = 256
    for j in range(m_ref.shape[1] // width):
        cols = pl.ds(j * width, width)
        low = mm(fblock, w_ref[:, cols], TN)
        rest = m_ref[:, cols].astype(F32) - low
        low_ref[:, cols] = low.astype(BF16)
        sparse_ref[:, cols] = (rest - jnp.clip(rest, -cutoff, cutoff)).astype(BF16)


def solution(mesh):
    nv, nf = mesh.shape["vox"], mesh.shape["frm"]

    def on_device(movie_matrix, voxel_probe, frame_probe):
        frames, voxels = movie_matrix.shape
        fb, vb = frames // nv, voxels // nf
        vmem = pl.BlockSpec(memory_space=pltpu.VMEM)
        dma = pltpu.SemaphoreType.DMA
        ft, w = pl.pallas_call(
            functools.partial(sketch_kernel, nv, nf),
            out_shape=(
                jax.ShapeDtypeStruct((nv, RANK, fb), BF16),
                jax.ShapeDtypeStruct((RANK, voxels), BF16),
            ),
            in_specs=[pl.BlockSpec(memory_space=pltpu.HBM), vmem, vmem],
            out_specs=(vmem, vmem),
            scratch_shapes=[
                pltpu.VMEM((frames, voxels), BF16),
                pltpu.VMEM((ITERS, nv, RANK, fb), BF16),
                pltpu.VMEM((ITERS, nv - 1, RANK, fb), BF16),
                pltpu.VMEM((ITERS, nv, RANK, fb), BF16),
                pltpu.VMEM((ITERS, nf, RANK, vb), BF16),
                pltpu.VMEM((ITERS, nf - 1, RANK, vb), BF16),
                pltpu.VMEM((ITERS, nf, RANK, vb), BF16),
                pltpu.VMEM((RANK, RANK), F32),
                pltpu.VMEM((ITERS, nf, 8, LANES), F32),
                pltpu.VMEM((ITERS, nf - 1, 8, LANES), F32),
                pltpu.VMEM((ITERS, 8, LANES), F32),
                pltpu.VMEM((ITERS, nv - 1, 8, LANES), F32),
                pltpu.VMEM((ITERS, nf, 8, LANES), F32),
                pltpu.VMEM((RANK, voxels), BF16),
                pltpu.VMEM((2, RANK, RANK), BF16),
                dma((nv // 2,)),
            ]
            + [dma((ITERS, 2))] * 7,
            compiler_params=pltpu.CompilerParams(
                collective_id=0, has_side_effects=True, vmem_limit_bytes=40 * 1024 * 1024
            ),
            name="sketches",
        )(movie_matrix, voxel_probe.T, frame_probe.T)
        per = 2
        rows = per * fb
        return pl.pallas_call(
            output_kernel,
            grid=(frames // rows,),
            out_shape=(
                jax.ShapeDtypeStruct((frames, voxels), BF16),
                jax.ShapeDtypeStruct((frames, voxels), BF16),
            ),
            in_specs=[
                pl.BlockSpec((rows, voxels), lambda i: (i, 0)),
                pl.BlockSpec((per, RANK, fb), lambda i: (i, 0, 0)),
                pl.BlockSpec((RANK, voxels), lambda i: (0, 0)),
            ],
            out_specs=(
                pl.BlockSpec((rows, voxels), lambda i: (i, 0)),
                pl.BlockSpec((rows, voxels), lambda i: (i, 0)),
            ),
            compiler_params=pltpu.CompilerParams(vmem_limit_bytes=24 * 1024 * 1024),
            name="outputs",
        )(movie_matrix, ft, w)

    return jax.shard_map(
        on_device,
        mesh=mesh,
        in_specs=(P("frm", "vox"), P("vox", None), P("frm", None)),
        out_specs=(P("frm", "vox"), P("frm", "vox")),
        check_vma=False,
    )
```

time: 211 us -> 80.8 us (0.38)
  Pallas kernels: 0 us -> 73.6 us
  waiting for transfers between devices: 57.3 us -> 0 us
  matrix products: 46.7 us -> 0 us
  starting transfers between devices: 45.9 us -> 0 us
  other arithmetic: 29.1 us -> 0 us
  blocking collectives: 13.9 us -> 0 us
  local copies, waits for them, and re-layouts: 14 us -> 5.27 us
    pallas_call x0 -> x2, Pallas kernels: none -> 73.6 us  [the longest x1 65.6 us: on_device(): pl.pallas_call(functools.partial(sketch_kernel, nv, nf), out_shape=(jax.S...]
    all_to_all x11 -> x0, waiting for transfers between devices: 57.3 us -> none  [the longest x8 36.2 us: copy_for_each(): return lax.all_to_all(copies, axis, split_axis=0, concat_axis=0, tiled=True)]
    dot_general x12 -> x0, matrix products: 45.9 us -> none  [the longest x2 24.8 us: on_device(): lax.dot_general(left_factor, right_factor, (((1,), (1,)), ((), ())), pref...]
    all_to_all x11 -> x0, starting transfers between devices: 45.9 us -> none  [the longest x8 29.2 us: copy_for_each(): return lax.all_to_all(copies, axis, split_axis=0, concat_axis=0, tiled=True)]
    another operation x10 -> x0, other arithmetic: 24.1 us -> none  [the longest x6 13 us: core_map(): jnp.linalg.cholesky(gram_matrix + ridge_shift * jnp.eye(core_order, dtype...]
    all_to_all x1 -> x0, blocking collectives: 13.9 us -> none  [sum_at_owner(): lax.all_to_all(tiles, axis, split_axis=0, concat_axis=0, tiled=True)]
    all_to_all x4 -> x0, other arithmetic: 4.6 us -> none  [copy_for_each(): return lax.all_to_all(copies, axis, split_axis=0, concat_axis=0, tiled=True)]
    broadcast_in_dim x8 -> x0, local copies, waits for them, and re-layouts: 3.07 us -> none  [copy_for_each(): copies = jnp.broadcast_to(x, (lax.axis_size(axis), *x.shape))]
  transfers between devices with their start and end apart: 11 -> 0, of which waited for: 9 -> 0; matrix products, arithmetic and copies ran while one was open for 22% -> 0% of each run, Pallas kernels for 0% -> 0%
where the time goes in v1:
time: 80.8 us; the launch traced here: 79.5 us
  Pallas kernels  73.6 us (91%)
  local copies, waits for them, and re-layouts  5.27 us (7%)
    pallas_call x1, Pallas kernels, on_device(): pl.pallas_call(functools.partial(sketch_kernel, nv, nf), out_shape=(jax.S...  65.6 us
    pallas_call x1, Pallas kernels, on_device(): pl.pallas_call(output_kernel, grid=(frames // rows,), out_shape=(jax.Shap...  7.99 us
    unnamed x6, local copies, waits for them, and re-layouts  5.27 us

profile of v1, /device:TPU:0, one launch (start us, length us, event | category | flops | bytes accessed | tf_op | source)
XLA Modules:
  0.0 79.5 jit_solution(8218100452266967498)
XLA Ops:
  0.6 0.0 copy-start
  0.6 3.4 %copy-done = bf16[2048,2048]{1,0:T(8,128)(2,1)S(1)} copy-done((bf16[2048,2048]{1,0:T(8,128)(2,1)S(1)}, bf16[2048,2048]{1,0:T(8,128)(2,1)}, u32[]{:S(2)}) %copy-start) | copy-done | bytes 8388632
  4.0 0.0 copy-start.1
  4.0 0.9 %copy-done.1 = bf16[2048,64]{0,1:T(8,128)(2,1)S(1)} copy-done((bf16[2048,64]{0,1:T(8,128)(2,1)S(1)}, bf16[2048,64]{0,1:T(8,128)(2,1)}, u32[]{:S(2)}) %copy-start.1) | copy-done | bytes 262168
  5.0 0.0 copy-start.2
  5.0 0.9 %copy-done.2 = bf16[2048,64]{0,1:T(8,128)(2,1)S(1)} copy-done((bf16[2048,64]{0,1:T(8,128)(2,1)S(1)}, bf16[2048,64]{0,1:T(8,128)(2,1)}, u32[]{:S(2)}) %copy-start.2) | copy-done | bytes 262168
  5.9 65.6 %sketches.1 = (bf16[16,64,128]{2,1,0:T(8,128)(2,1)S(1)}, bf16[64,2048]{1,0:T(8,128)(2,1)S(1)}) custom-call(bf16[2048,2048]{1,0:T(8,128)(2,1)S(1)} %copy-done, bf16[64,2048]{1,0:T(8,128)(2,1)S(1)} %bitcast.2, bf16[64,2048]{1,0:T(8,128)(2,1)S(1)} %bitcast.3), custom_call_target="tpu_custom_call" | custom-call | tf_op jit(solution)/shard_map/sketches/pallas_call | solution.py:257
  71.5 8.0 %outputs.1 = (bf16[2048,2048]{1,0:T(8,128)(2,1)}, bf16[2048,2048]{1,0:T(8,128)(2,1)}) custom-call(bf16[2048,2048]{1,0:T(8,128)(2,1)S(1)} %copy-done, bf16[16,64,128]{2,1,0:T(8,128)(2,1)S(1)} %get-tuple-element.4.ft_ref, bf16[64,2048]{1,0:T(8,128)(2,1)S(1)} %get-tuple-element.5.w_ref), custom_call_target="tpu_custom_call" | custom-call | tf_op jit(solution)/shard_map/outputs/pallas_call | solution.py:291
Async XLA Ops:
  0.6 3.4 %copy-start = (bf16[2048,2048]{1,0:T(8,128)(2,1)S(1)}, bf16[2048,2048]{1,0:T(8,128)(2,1)}, u32[]{:S(2)}) copy-start(bf16[2048,2048]{1,0:T(8,128)(2,1)} %m_ref.1) | copy-start | bytes 25165828
  4.0 0.9 %copy-start.1 = (bf16[2048,64]{0,1:T(8,128)(2,1)S(1)}, bf16[2048,64]{0,1:T(8,128)(2,1)}, u32[]{:S(2)}) copy-start(bf16[2048,64]{0,1:T(8,128)(2,1)} %param.4) | copy-start | bytes 786436
  5.0 0.9 %copy-start.2 = (bf16[2048,64]{0,1:T(8,128)(2,1)S(1)}, bf16[2048,64]{0,1:T(8,128)(2,1)}, u32[]{:S(2)}) copy-start(bf16[2048,64]{0,1:T(8,128)(2,1)} %param.5) | copy-start | bytes 786436

commit v2 on v1

v2 whole, which is shorter than its diff:
```python
import functools

import jax
import jax.numpy as jnp
from jax import lax
from jax.experimental import pallas as pl
from jax.experimental.pallas import tpu as pltpu
from jax.sharding import PartitionSpec as P

MESH = pl.DeviceIdType.MESH
BF16, F32 = jnp.bfloat16, jnp.float32
ITERS = 2
RANK = 64
HALF = RANK // 2
SUB, LANES = 8, 128
cutoff = 1.0
ridge_scale = 0.1
NN = (((1,), (0,)), ((), ()))
NT = (((1,), (1,)), ((), ()))


def mm(a, b, dims):
    return lax.dot_general(a, b, dims, preferred_element_type=F32)


def split(x):
    high = x.astype(BF16)
    return high, (x - high.astype(F32)).astype(BF16)


def spread(x):
    return jnp.broadcast_to(x, (SUB, LANES))


def eliminate(panel, base):
    columns = [spread(panel[:, base + j : base + j + 1]) for j in range(SUB)]
    e = [[spread(columns[j][i : i + 1, :]) for j in range(SUB)] for i in range(SUB)]
    rows = [spread(panel[i : i + 1, :]) for i in range(SUB)]
    for k in range(0, SUB, 2):
        a, b, d = e[k][k], e[k][k + 1], e[k + 1][k + 1]
        r = 1.0 / (a * d - b * b)
        first, cross, last = d * r, b * r, a * r

        def pair(x, y):
            return first * x - cross * y, last * y - cross * x

        rows[k], rows[k + 1] = pair(rows[k], rows[k + 1])
        for j in range(k + 2, SUB):
            e[k][j], e[k + 1][j] = pair(e[k][j], e[k + 1][j])
        for i in range(SUB):
            if i in (k, k + 1):
                continue
            p, q = e[i][k], e[i][k + 1]
            rows[i] = rows[i] - p * rows[k] - q * rows[k + 1]
            for j in range(k + 2, SUB):
                e[i][j] = e[i][j] - p * e[k][j] - q * e[k + 1][j]
    return rows


def solve(blocks, base):
    row_id = lax.broadcasted_iota(jnp.int32, (SUB, LANES), 0)
    blocks, n = list(blocks), len(blocks)
    for b in range(n):
        at = base + SUB * b
        rows = eliminate(blocks[b], at)
        for j in [(b + 1 + i) % n for i in range(n - 1)]:
            terms = [spread(blocks[j][:, at + k : at + k + 1]) * rows[k] for k in range(SUB)]
            while len(terms) > 1:
                terms = [x + y for x, y in zip(terms[::2], terms[1::2])]
            blocks[j] = blocks[j] - terms[0]
        panel = rows[SUB - 1]
        for k in range(SUB - 1):
            panel = jnp.where(row_id == k, rows[k], panel)
        blocks[b] = panel
    return blocks


def square(t):
    first, rest = t.astype(BF16), t - t.astype(BF16).astype(F32)
    second, third = rest.astype(BF16), (rest - rest.astype(BF16).astype(F32)).astype(BF16)
    tall = [jnp.concatenate([jnp.zeros_like(x), x], axis=0) for x in (first, second, third)]
    small = mm(first, tall[2], NT) + mm(third, tall[0], NT) + mm(second, tall[1], NT)
    return small + (mm(first, tall[1], NT) + mm(second, tall[0], NT)) + mm(first, tall[0], NT)


def mixer_of(t):
    shift = ridge_scale * (jnp.sum(t * t) / RANK + 1e-06)
    rows = lax.broadcasted_iota(jnp.int32, t.shape, 0)
    lanes = lax.broadcasted_iota(jnp.int32, t.shape, 1)
    wide = square(t) + t + jnp.where(rows + RANK == lanes, shift, 0.0)
    blocks = solve([wide[SUB * b : SUB * b + SUB] for b in range(RANK // SUB)], RANK)
    return jnp.concatenate(blocks, axis=0)


def sketch_kernel(
    nv, nf, fc, vc,
    m_hbm, vp_hbm, fp_hbm, m_buf, ft_out, w_buf,
    c_buf, vpt, fpt, f_send, f_recv, ft_full, v_send, v_recv, vt_full, t_acc, t_mine, t_recv, t_sum, t_wide, mix,
    m_sem, p_sem, f_sem, fg_sem, v_sem, vg_sem, ta_sem, tb_sem,
):
    mv, mf = lax.axis_index("vox"), lax.axis_index("frm")
    frames, voxels = m_buf.shape
    fb, vb = frames // nv, voxels // nf
    rows, columns = fb * fc, vb * vc
    row_chunks, column_chunks = nv // fc, nf // vc

    def row_chunk(s):
        return lax.rem(mv // fc + 1 + s, row_chunks)

    def rows_of(c):
        return pl.ds(pl.multiple_of(c * rows, rows), rows)

    def load(s):
        at = rows_of(row_chunk(s))
        return pltpu.make_async_copy(m_hbm.at[at], m_buf.at[at], m_sem.at[s])

    vp_load = pltpu.make_async_copy(vp_hbm, vpt, p_sem.at[0])
    fp_load = pltpu.make_async_copy(fp_hbm, fpt, p_sem.at[1])
    vp_load.start()
    load(0).start()
    fp_load.start()
    for s in range(1, row_chunks):
        load(s).start()

    barrier = pltpu.get_barrier_semaphore()
    for d in range(1, nv):
        pl.semaphore_signal(barrier, inc=1, device_id={"vox": lax.rem(mv + d, nv)}, device_id_type=MESH)
    for d in range(1, nf):
        pl.semaphore_signal(barrier, inc=1, device_id={"frm": lax.rem(mf + d, nf)}, device_id_type=MESH)

    def to(axis, src, dst, sems, it, target):
        return pltpu.make_async_remote_copy(
            src_ref=src, dst_ref=dst, send_sem=sems.at[it, 0], recv_sem=sems.at[it, 1],
            device_id={axis: target}, device_id_type=MESH,
        )

    def vox_peer(d):
        return lax.rem(mv + d, nv)

    def frm_peer(d):
        return lax.rem(mf + d, nf)

    def f_to(it, owner):
        slot = lax.rem(owner - mv + nv, nv) - 1
        return to("vox", f_send.at[it, owner], f_recv.at[it, slot], f_sem, it, owner)

    def v_to(it, owner):
        slot = lax.rem(owner - mf + nf, nf) - 1
        return to("frm", v_send.at[it, owner], v_recv.at[it, slot], v_sem, it, owner)

    def whole(kind, it):
        if kind == "f":
            return to("vox", f_recv.at[it], f_recv.at[it], f_sem, it, vox_peer(1))
        if kind == "fg":
            part = ft_full.at[it, pl.ds(0, nv - 1)]
            return to("vox", part, part, fg_sem, it, vox_peer(1))
        if kind == "v":
            return to("frm", v_recv.at[it], v_recv.at[it], v_sem, it, frm_peer(1))
        if kind == "vg":
            part = vt_full.at[it, pl.ds(0, nf - 1)]
            return to("frm", part, part, vg_sem, it, frm_peer(1))
        if kind == "ta":
            return to("frm", t_recv.at[it], t_recv.at[it], ta_sem, it, frm_peer(1))
        return to("vox", t_wide.at[it], t_wide.at[it], tb_sem, it, vox_peer(1))

    for it in range(ITERS):
        src = m_buf if it == 0 else c_buf

        def frame_step(s, carry):
            c = row_chunk(s)
            if it == 0:
                load(s).wait()
            else:
                left = jnp.concatenate([ft_full[it - 1, fc * c + i] for i in range(fc)], axis=1).T
                for j in range(voxels // WIDE):
                    at = (rows_of(c), pl.ds(j * WIDE, WIDE))
                    low = mm(left, w_buf[:, at[1]], NN)
                    floor, roof = (low - cutoff).astype(BF16), (low + cutoff).astype(BF16)
                    c_buf[at] = jnp.minimum(jnp.maximum(m_buf[at], floor), roof)
            ft = mm(vpt[...], src[rows_of(c), :], NT)
            high, low_part = split(ft)
            for i in range(fc):
                f_send[it, fc * c + i] = high[:, i * fb : (i + 1) * fb]
            probe = fpt[:, rows_of(c)]
            t_acc[...] += mm(high, probe, NT) + mm(low_part, probe, NT)
            if it > 0:
                for i in range(fc):
                    owner = fc * c + i

                    @pl.when(owner != mv)
                    def _():
                        f_to(it, owner).start()

            return carry

        t_acc[...] = jnp.zeros_like(t_acc)
        if it == 0:
            vp_load.wait()
            fp_load.wait()
        lax.fori_loop(0, row_chunks, frame_step, 0)

        t_mine[it] = jnp.concatenate([t_acc[:HALF, :], t_acc[HALF:, :]], axis=1)
        if it == 0:
            pl.semaphore_wait(barrier, nv + nf - 2)
        for d in range(1, nf):
            to("frm", t_mine.at[it], t_recv.at[it, d - 1], ta_sem, it, frm_peer(d)).start()
        if it == 0:
            for d in range(1, nv):
                f_to(it, vox_peer(d)).start()

        def voxel_step(s, carry):
            c = lax.rem(mf // vc + 1 + s, column_chunks)
            at = pl.ds(pl.multiple_of(c * columns, columns), columns)
            vt = mm(fpt[...], src[:, at], NN).astype(BF16)
            for i in range(vc):
                owner = vc * c + i
                v_send[it, owner] = vt[:, i * vb : (i + 1) * vb]

                @pl.when(owner != mf)
                def _():
                    v_to(it, owner).start()

            return carry

        lax.fori_loop(0, column_chunks, voxel_step, 0)

        whole("ta", it).wait_recv()
        part = t_mine[it]
        for d in range(nf - 1):
            part = part + t_recv[it, d]
        t_sum[it] = part
        for d in range(1, nv):
            to("vox", t_sum.at[it], t_wide.at[it, d - 1], tb_sem, it, vox_peer(d)).start()

        whole("f", it).wait_recv()
        share = f_send[it, mv].astype(F32)
        for d in range(nv - 1):
            share = share + f_recv[it, d].astype(F32)
        ft_full[it, mv] = share.astype(BF16)
        for d in range(1, nv):
            to("vox", ft_full.at[it, mv], ft_full.at[it, mv], fg_sem, it, vox_peer(d)).start()

        whole("v", it).wait_recv()
        share = v_send[it, mf].astype(F32)
        for d in range(nf - 1):
            share = share + v_recv[it, d].astype(F32)
        vt_full[it, mf] = share.astype(BF16)
        for d in range(1, nf):
            to("frm", vt_full.at[it, mf], vt_full.at[it, mf], vg_sem, it, frm_peer(d)).start()

        whole("tb", it).wait_recv()
        part = t_sum[it]
        for d in range(nv - 1):
            part = part + t_wide[it, d]
        lanes = lax.broadcasted_iota(jnp.int32, part.shape, 1)
        left_half = jnp.where(lanes < RANK, part, 0.0)
        right_half = pltpu.roll(jnp.where(lanes < RANK, 0.0, part), RANK, 1)
        mixer = mixer_of(jnp.concatenate([left_half, right_half], axis=0))
        mix[0], mix[1] = split(mixer)

        whole("vg", it).wait_recv()
        for b in range(nf):
            right = vt_full[it, b]
            w = mm(mix[0, :, :RANK], right, NN) + mm(mix[1, :, :RANK], right, NN)
            w_buf[:, b * vb : (b + 1) * vb] = w.astype(BF16)
        whole("fg", it).wait_recv()

    ft_out[...] = ft_full[ITERS - 1]
    for it in range(ITERS):
        for kind in ("f", "fg", "v", "vg", "ta", "tb"):
            whole(kind, it).wait_send()


WIDE = 512


def output_kernel(rows, m_ref, ft_ref, w_ref, low_ref, sparse_ref):
    at = pl.ds(pl.multiple_of(pl.program_id(0) * rows, rows), rows)
    left = jnp.concatenate([ft_ref[i] for i in range(ft_ref.shape[0])], axis=1).T
    for j in range(m_ref.shape[1] // WIDE):
        cols = pl.ds(j * WIDE, WIDE)
        low = mm(left, w_ref[:, cols], NN)
        rest = m_ref[at, cols].astype(F32) - low
        low_ref[:, cols] = low.astype(BF16)
        sparse_ref[:, cols] = (rest - jnp.clip(rest, -cutoff, cutoff)).astype(BF16)


def solution(mesh):
    nv, nf = mesh.shape["vox"], mesh.shape["frm"]

    def on_device(movie_matrix, voxel_probe, frame_probe):
        frames, voxels = movie_matrix.shape
        fb, vb = frames // nv, voxels // nf
        vmem = pl.BlockSpec(memory_space=pltpu.VMEM)
        hbm = pl.BlockSpec(memory_space=pltpu.HBM)
        dma = pltpu.SemaphoreType.DMA
        fc, vc = 4, 2
        movie, ft, w = pl.pallas_call(
            functools.partial(sketch_kernel, nv, nf, fc, vc),
            out_shape=(
                jax.ShapeDtypeStruct((frames, voxels), BF16),
                jax.ShapeDtypeStruct((nv, RANK, fb), BF16),
                jax.ShapeDtypeStruct((RANK, voxels), BF16),
            ),
            in_specs=[hbm, hbm, hbm],
            out_specs=(vmem, vmem, vmem),
            scratch_shapes=[
                pltpu.VMEM((frames, voxels), BF16),
                pltpu.VMEM((RANK, voxels), BF16),
                pltpu.VMEM((RANK, frames), BF16),
                pltpu.VMEM((ITERS, nv, RANK, fb), BF16),
                pltpu.VMEM((ITERS, nv - 1, RANK, fb), BF16),
                pltpu.VMEM((ITERS, nv, RANK, fb), BF16),
                pltpu.VMEM((ITERS, nf, RANK, vb), BF16),
                pltpu.VMEM((ITERS, nf - 1, RANK, vb), BF16),
                pltpu.VMEM((ITERS, nf, RANK, vb), BF16),
                pltpu.VMEM((RANK, RANK), F32),
                pltpu.VMEM((ITERS, HALF, LANES), F32),
                pltpu.VMEM((ITERS, nf - 1, HALF, LANES), F32),
                pltpu.VMEM((ITERS, HALF, LANES), F32),
                pltpu.VMEM((ITERS, nv - 1, HALF, LANES), F32),
                pltpu.VMEM((2, RANK, LANES), BF16),
                dma((nv // fc,)),
                dma((2,)),
            ]
            + [dma((ITERS, 2))] * 6,
            compiler_params=pltpu.CompilerParams(
                collective_id=0, has_side_effects=True, vmem_limit_bytes=40 * 1024 * 1024
            ),
            name="sketches",
        )(movie_matrix, voxel_probe.T, frame_probe.T)
        per = 2
        rows = per * fb
        block = pl.BlockSpec((rows, voxels), lambda i: (i, 0))
        return pl.pallas_call(
            functools.partial(output_kernel, rows),
            grid=(frames // rows,),
            out_shape=(
                jax.ShapeDtypeStruct((frames, voxels), BF16),
                jax.ShapeDtypeStruct((frames, voxels), BF16),
            ),
            in_specs=[vmem, pl.BlockSpec((per, RANK, fb), lambda i: (i, 0, 0)), vmem],
            out_specs=(block, block),
            compiler_params=pltpu.CompilerParams(vmem_limit_bytes=24 * 1024 * 1024),
            name="outputs",
        )(movie, ft, w)

    return jax.shard_map(
        on_device,
        mesh=mesh,
        in_specs=(P("frm", "vox"), P("vox", None), P("frm", None)),
        out_specs=(P("frm", "vox"), P("frm", "vox")),
        check_vma=False,
    )
```

time: 80.8 us -> 54 us (0.67); the launches traced: 79.5 us -> 53.7 us
  Pallas kernels: 73.6 us -> 51.2 us
  local copies, waits for them, and re-layouts: 5.27 us -> 1.89 us
    pallas_call x2, Pallas kernels: 73.6 us -> 51.2 us  [the longest x1 43.2 us: on_device(): pl.pallas_call(functools.partial(sketch_kernel, nv, nf, fc, vc), out_shap...]
    unnamed x6 -> x4, local copies, waits for them, and re-layouts: 5.27 us -> 1.89 us
where the time goes in v2:
time: 54 us; the launch traced here: 53.7 us
  Pallas kernels  51.2 us (95%)
  local copies, waits for them, and re-layouts  1.89 us (4%)
  between operations  0.65 us (1%)
    pallas_call x1, Pallas kernels, on_device(): pl.pallas_call(functools.partial(sketch_kernel, nv, nf, fc, vc), out_shap...  43.2 us
    pallas_call x1, Pallas kernels, on_device(): pl.pallas_call(functools.partial(output_kernel, rows), grid=(frames // ro...  7.99 us
    unnamed x4, local copies, waits for them, and re-layouts  1.89 us

profile of v2, /device:TPU:0, one launch (start us, length us, event | category | flops | bytes accessed | tf_op | source)
XLA Modules:
  0.0 53.7 jit_solution(15359888045537868636)
XLA Ops:
  0.6 0.0 copy-start
  0.6 0.9 %copy-done = bf16[2048,64]{0,1:T(8,128)(2,1)S(1)} copy-done((bf16[2048,64]{0,1:T(8,128)(2,1)S(1)}, bf16[2048,64]{0,1:T(8,128)(2,1)}, u32[]{:S(2)}) %copy-start) | copy-done | bytes 262168
  1.6 0.0 copy-start.1
  1.6 0.9 %copy-done.1 = bf16[2048,64]{0,1:T(8,128)(2,1)S(1)} copy-done((bf16[2048,64]{0,1:T(8,128)(2,1)S(1)}, bf16[2048,64]{0,1:T(8,128)(2,1)}, u32[]{:S(2)}) %copy-start.1) | copy-done | bytes 262168
  2.5 43.2 %sketches.1 = (bf16[2048,2048]{1,0:T(8,128)(2,1)S(1)}, bf16[16,64,128]{2,1,0:T(8,128)(2,1)S(1)}, bf16[64,2048]{1,0:T(8,128)(2,1)S(1)}) custom-call(bf16[2048,2048]{1,0:T(8,128)(2,1)} %m_hbm.1, bf16[64,2048]{1,0:T(8,128)(2,1)S(1)} %bitcast.2, bf16[64,2048]{1,0:T(8,128)(2,1)S(1)} %bitcast.3), custom_call_target="tpu_custom_call" | custom-call | tf_op jit(solution)/shard_map/sketches/pallas_call | solution.py:298
  45.7 8.0 %outputs.1 = (bf16[2048,2048]{1,0:T(8,128)(2,1)}, bf16[2048,2048]{1,0:T(8,128)(2,1)}) custom-call(bf16[2048,2048]{1,0:T(8,128)(2,1)S(1)} %get-tuple-element.5.m_ref, bf16[16,64,128]{2,1,0:T(8,128)(2,1)S(1)} %get-tuple-element.6.ft_ref, bf16[64,2048]{1,0:T(8,128)(2,1)S(1)} %get-tuple-element.7.w_ref), custom_call_target="tpu_custom_call" | custom-call | tf_op jit(solution)/shard_map/outputs/pallas_call | solution.py:335
Async XLA Ops:
  0.6 1.0 %copy-start = (bf16[2048,64]{0,1:T(8,128)(2,1)S(1)}, bf16[2048,64]{0,1:T(8,128)(2,1)}, u32[]{:S(2)}) copy-start(bf16[2048,64]{0,1:T(8,128)(2,1)} %param.4) | copy-start | bytes 786436
  1.6 0.9 %copy-start.1 = (bf16[2048,64]{0,1:T(8,128)(2,1)S(1)}, bf16[2048,64]{0,1:T(8,128)(2,1)}, u32[]{:S(2)}) copy-start(bf16[2048,64]{0,1:T(8,128)(2,1)} %param.5) | copy-start | bytes 786436

commit v3 on v2

--- a/solution.py
+++ b/solution.py
@@ -12,6 +12,7 @@
 ITERS = 2
 RANK = 64
 HALF = RANK // 2
+WIDE = 256
 SUB, LANES = 8, 128
 cutoff = 1.0
 ridge_scale = 0.1
@@ -92,8 +93,16 @@
     return jnp.concatenate(blocks, axis=0)
 
 
+def far_first(n, inner):
+    def hops(d):
+        outer = n // inner
+        return min(d // inner, outer - d // inner) + min(d % inner, inner - d % inner)
+
+    return sorted(range(1, n), key=lambda d: -hops(d))
+
+
 def sketch_kernel(
-    nv, nf, fc, vc,
+    nv, nf, side, cores, fc, vc,
     m_hbm, vp_hbm, fp_hbm, m_buf, ft_out, w_buf,
     c_buf, vpt, fpt, f_send, f_recv, ft_full, v_send, v_recv, vt_full, t_acc, t_mine, t_recv, t_sum, t_wide, mix,
     m_sem, p_sem, f_sem, fg_sem, v_sem, vg_sem, ta_sem, tb_sem,
@@ -122,11 +131,18 @@
     for s in range(1, row_chunks):
         load(s).start()
 
+    def vox_peer(d):
+        return (mv // side + d // side) % (nv // side) * side + (mv + d) % side
+
+    def frm_peer(d):
+        return (mf // cores + d // cores) % (nf // cores) * cores + (mf + d) % cores
+
+    vox_order, frm_order = far_first(nv, side), far_first(nf, cores)
     barrier = pltpu.get_barrier_semaphore()
-    for d in range(1, nv):
-        pl.semaphore_signal(barrier, inc=1, device_id={"vox": lax.rem(mv + d, nv)}, device_id_type=MESH)
-    for d in range(1, nf):
-        pl.semaphore_signal(barrier, inc=1, device_id={"frm": lax.rem(mf + d, nf)}, device_id_type=MESH)
+    for d in vox_order:
+        pl.semaphore_signal(barrier, inc=1, device_id={"vox": vox_peer(d)}, device_id_type=MESH)
+    for d in frm_order:
+        pl.semaphore_signal(barrier, inc=1, device_id={"frm": frm_peer(d)}, device_id_type=MESH)
 
     def to(axis, src, dst, sems, it, target):
         return pltpu.make_async_remote_copy(
@@ -134,18 +150,12 @@
             device_id={axis: target}, device_id_type=MESH,
         )
 
-    def vox_peer(d):
-        return lax.rem(mv + d, nv)
-
-    def frm_peer(d):
-        return lax.rem(mf + d, nf)
-
     def f_to(it, owner):
-        slot = lax.rem(owner - mv + nv, nv) - 1
+        slot = (owner // side - mv // side + nv // side) % (nv // side) * side + (owner - mv + nv) % side - 1
         return to("vox", f_send.at[it, owner], f_recv.at[it, slot], f_sem, it, owner)
 
     def v_to(it, owner):
-        slot = lax.rem(owner - mf + nf, nf) - 1
+        slot = (owner // cores - mf // cores + nf // cores) % (nf // cores) * cores + (owner - mf + nf) % cores - 1
         return to("frm", v_send.at[it, owner], v_recv.at[it, slot], v_sem, it, owner)
 
     def whole(kind, it):
@@ -202,10 +212,10 @@
         t_mine[it] = jnp.concatenate([t_acc[:HALF, :], t_acc[HALF:, :]], axis=1)
         if it == 0:
             pl.semaphore_wait(barrier, nv + nf - 2)
-        for d in range(1, nf):
+        for d in frm_order:
             to("frm", t_mine.at[it], t_recv.at[it, d - 1], ta_sem, it, frm_peer(d)).start()
         if it == 0:
-            for d in range(1, nv):
+            for d in vox_order:
                 f_to(it, vox_peer(d)).start()
 
         def voxel_step(s, carry):
@@ -229,7 +239,7 @@
         for d in range(nf - 1):
             part = part + t_recv[it, d]
         t_sum[it] = part
-        for d in range(1, nv):
+        for d in vox_order:
             to("vox", t_sum.at[it], t_wide.at[it, d - 1], tb_sem, it, vox_peer(d)).start()
 
         whole("f", it).wait_recv()
@@ -237,7 +247,7 @@
         for d in range(nv - 1):
             share = share + f_recv[it, d].astype(F32)
         ft_full[it, mv] = share.astype(BF16)
-        for d in range(1, nv):
+        for d in vox_order:
             to("vox", ft_full.at[it, mv], ft_full.at[it, mv], fg_sem, it, vox_peer(d)).start()
 
         whole("v", it).wait_recv()
@@ -245,7 +255,7 @@
         for d in range(nf - 1):
             share = share + v_recv[it, d].astype(F32)
         vt_full[it, mf] = share.astype(BF16)
-        for d in range(1, nf):
+        for d in frm_order:
             to("frm", vt_full.at[it, mf], vt_full.at[it, mf], vg_sem, it, frm_peer(d)).start()
 
         whole("tb", it).wait_recv()
@@ -271,18 +281,34 @@
             whole(kind, it).wait_send()
 
 
-WIDE = 512
-
-
-def output_kernel(rows, m_ref, ft_ref, w_ref, low_ref, sparse_ref):
-    at = pl.ds(pl.multiple_of(pl.program_id(0) * rows, rows), rows)
-    left = jnp.concatenate([ft_ref[i] for i in range(ft_ref.shape[0])], axis=1).T
-    for j in range(m_ref.shape[1] // WIDE):
-        cols = pl.ds(j * WIDE, WIDE)
-        low = mm(left, w_ref[:, cols], NN)
-        rest = m_ref[at, cols].astype(F32) - low
-        low_ref[:, cols] = low.astype(BF16)
-        sparse_ref[:, cols] = (rest - jnp.clip(rest, -cutoff, cutoff)).astype(BF16)
+def output_kernel(per, m_ref, ft_ref, w_ref, low_hbm, sparse_hbm, low_buf, sparse_buf, sems):
+    slots, rows, voxels = low_buf.shape
+    steps = ft_ref.shape[0] // per
+
+    def copies(i):
+        at, k = pl.ds(i * rows, rows), i % slots
+        return (
+            pltpu.make_async_copy(low_buf.at[k], low_hbm.at[at], sems.at[0, k]),
+            pltpu.make_async_copy(sparse_buf.at[k], sparse_hbm.at[at], sems.at[1, k]),
+        )
+
+    for i in range(steps):
+        k = i % slots
+        if i >= slots:
+            for copy in copies(i - slots):
+                copy.wait()
+        left = jnp.concatenate([ft_ref[per * i + q] for q in range(per)], axis=1).T
+        for j in range(voxels // WIDE):
+            cols = pl.ds(j * WIDE, WIDE)
+            low = mm(left, w_ref[:, cols], NN)
+            rest = m_ref[pl.ds(i * rows, rows), cols].astype(F32) - low
+            low_buf[k, :, cols] = low.astype(BF16)
+            sparse_buf[k, :, cols] = (rest - jnp.clip(rest, -cutoff, cutoff)).astype(BF16)
+        for copy in copies(i):
+            copy.start()
+    for i in range(steps - slots, steps):
+        for copy in copies(i):
+            copy.wait()
 
 
 def solution(mesh):
@@ -294,9 +320,9 @@
         vmem = pl.BlockSpec(memory_space=pltpu.VMEM)
         hbm = pl.BlockSpec(memory_space=pltpu.HBM)
         dma = pltpu.SemaphoreType.DMA
-        fc, vc = 4, 2
+        fc, vc = nv // 2, nf // 2
         movie, ft, w = pl.pallas_call(
-            functools.partial(sketch_kernel, nv, nf, fc, vc),
+            functools.partial(sketch_kernel, nv, nf, 4, 2, fc, vc),
             out_shape=(
                 jax.ShapeDtypeStruct((frames, voxels), BF16),
                 jax.ShapeDtypeStruct((nv, RANK, fb), BF16),
@@ -328,19 +354,21 @@
                 collective_id=0, has_side_effects=True, vmem_limit_bytes=40 * 1024 * 1024
             ),
             name="sketches",
-        )(movie_matrix, voxel_probe.T, frame_probe.T)
-        per = 2
-        rows = per * fb
-        block = pl.BlockSpec((rows, voxels), lambda i: (i, 0))
+        )(
+            movie_matrix,
+            pltpu.with_memory_space_constraint(voxel_probe.T, pltpu.HBM),
+            pltpu.with_memory_space_constraint(frame_probe.T, pltpu.HBM),
+        )
+        per, slots = 2, 4
         return pl.pallas_call(
-            functools.partial(output_kernel, rows),
-            grid=(frames // rows,),
+            functools.partial(output_kernel, per),
             out_shape=(
                 jax.ShapeDtypeStruct((frames, voxels), BF16),
                 jax.ShapeDtypeStruct((frames, voxels), BF16),
             ),
-            in_specs=[vmem, pl.BlockSpec((per, RANK, fb), lambda i: (i, 0, 0)), vmem],
-            out_specs=(block, block),
+            in_specs=[vmem, vmem, vmem],
+            out_specs=(hbm, hbm),
+            scratch_shapes=[pltpu.VMEM((slots, per * fb, voxels), BF16)] * 2 + [dma((2, slots))],
             compiler_params=pltpu.CompilerParams(vmem_limit_bytes=24 * 1024 * 1024),
             name="outputs",
         )(movie, ft, w)

time: 54 us -> 50.4 us (0.933)
  local copies, waits for them, and re-layouts: 1.89 us -> 0 us
  Pallas kernels: 51.2 us -> 49.5 us
    unnamed x4 -> x0, local copies, waits for them, and re-layouts: 1.89 us -> none
    pallas_call x2, Pallas kernels: 51.2 us -> 49.5 us  [the longest x1 43 us: on_device(): pl.pallas_call(functools.partial(sketch_kernel, nv, nf, 4, 2, fc, vc), ou...]
where the time goes in v3:
time: 50.4 us; the launch traced here: 50.3 us
  Pallas kernels  49.5 us (98%)
  between operations  0.8 us (2%)
    pallas_call x1, Pallas kernels, on_device(): pl.pallas_call(functools.partial(sketch_kernel, nv, nf, 4, 2, fc, vc), ou...  43 us
    pallas_call x1, Pallas kernels, on_device(): pl.pallas_call(functools.partial(output_kernel, per), out_shape=(jax.Shap...  6.47 us

profile of v3, /device:TPU:0, one launch (start us, length us, event | category | flops | bytes accessed | tf_op | source)
XLA Modules:
  0.0 50.3 jit_solution(14392481289088037089)
XLA Ops:
  0.6 43.0 %sketches.1 = (bf16[2048,2048]{1,0:T(8,128)(2,1)S(1)}, bf16[16,64,128]{2,1,0:T(8,128)(2,1)S(1)}, bf16[64,2048]{1,0:T(8,128)(2,1)S(1)}) custom-call(bf16[2048,2048]{1,0:T(8,128)(2,1)} %m_hbm.1, bf16[64,2048]{1,0:T(8,128)(2,1)} %bitcast.2, bf16[64,2048]{1,0:T(8,128)(2,1)} %bitcast.3), custom_call_target="tpu_custom_call" | custom-call | tf_op jit(solution)/shard_map/sketches/pallas_call | solution.py:324
  43.6 6.5 %outputs.1 = (bf16[2048,2048]{1,0:T(8,128)(2,1)}, bf16[2048,2048]{1,0:T(8,128)(2,1)}) custom-call(bf16[2048,2048]{1,0:T(8,128)(2,1)S(1)} %get-tuple-element.5.m_ref, bf16[16,64,128]{2,1,0:T(8,128)(2,1)S(1)} %get-tuple-element.6.ft_ref, bf16[64,2048]{1,0:T(8,128)(2,1)S(1)} %get-tuple-element.7.w_ref), custom_call_target="tpu_custom_call" | custom-call | tf_op jit(solution)/shard_map/outputs/pallas_call | solution.py:363

commit v4 on v3

--- a/solution.py
+++ b/solution.py
@@ -33,9 +33,11 @@
     return jnp.broadcast_to(x, (SUB, LANES))
 
 
-def eliminate(panel, base):
-    columns = [spread(panel[:, base + j : base + j + 1]) for j in range(SUB)]
-    e = [[spread(columns[j][i : i + 1, :]) for j in range(SUB)] for i in range(SUB)]
+def eliminate(panel, base, keep):
+    for j in range(SUB):
+        keep[j] = spread(panel[:, base + j : base + j + 1])
+    upper = {(i, j): spread(keep[j, i : i + 1, :]) for j in range(SUB) for i in range(j + 1)}
+    e = [[upper[min(i, j), max(i, j)] for j in range(SUB)] for i in range(SUB)]
     rows = [spread(panel[i : i + 1, :]) for i in range(SUB)]
     for k in range(0, SUB, 2):
         a, b, d = e[k][k], e[k][k + 1], e[k + 1][k + 1]
@@ -58,12 +60,12 @@
     return rows
 
 
-def solve(blocks, base):
+def solve(blocks, base, keep):
     row_id = lax.broadcasted_iota(jnp.int32, (SUB, LANES), 0)
     blocks, n = list(blocks), len(blocks)
     for b in range(n):
         at = base + SUB * b
-        rows = eliminate(blocks[b], at)
+        rows = eliminate(blocks[b], at, keep.at[b])
         for j in [(b + 1 + i) % n for i in range(n - 1)]:
             terms = [spread(blocks[j][:, at + k : at + k + 1]) * rows[k] for k in range(SUB)]
             while len(terms) > 1:
@@ -84,12 +86,12 @@
     return small + (mm(first, tall[1], NT) + mm(second, tall[0], NT)) + mm(first, tall[0], NT)
 
 
-def mixer_of(t):
+def mixer_of(t, keep):
     shift = ridge_scale * (jnp.sum(t * t) / RANK + 1e-06)
     rows = lax.broadcasted_iota(jnp.int32, t.shape, 0)
     lanes = lax.broadcasted_iota(jnp.int32, t.shape, 1)
     wide = square(t) + t + jnp.where(rows + RANK == lanes, shift, 0.0)
-    blocks = solve([wide[SUB * b : SUB * b + SUB] for b in range(RANK // SUB)], RANK)
+    blocks = solve([wide[SUB * b : SUB * b + SUB] for b in range(RANK // SUB)], RANK, keep)
     return jnp.concatenate(blocks, axis=0)
 
 
@@ -104,7 +106,7 @@
 def sketch_kernel(
     nv, nf, side, cores, fc, vc,
     m_hbm, vp_hbm, fp_hbm, m_buf, ft_out, w_buf,
-    c_buf, vpt, fpt, f_send, f_recv, ft_full, v_send, v_recv, vt_full, t_acc, t_mine, t_recv, t_sum, t_wide, mix,
+    c_buf, vpt, fpt, f_send, f_recv, ft_full, v_send, v_recv, vt_full, t_acc, t_mine, t_recv, t_sum, t_wide, mix, keep,
     m_sem, p_sem, f_sem, fg_sem, v_sem, vg_sem, ta_sem, tb_sem,
 ):
     mv, mf = lax.axis_index("vox"), lax.axis_index("frm")
@@ -265,13 +267,15 @@
         lanes = lax.broadcasted_iota(jnp.int32, part.shape, 1)
         left_half = jnp.where(lanes < RANK, part, 0.0)
         right_half = pltpu.roll(jnp.where(lanes < RANK, 0.0, part), RANK, 1)
-        mixer = mixer_of(jnp.concatenate([left_half, right_half], axis=0))
-        mix[0], mix[1] = split(mixer)
+        mixer = mixer_of(jnp.concatenate([left_half, right_half], axis=0), keep)
+        high, low_part = split(mixer)
+        both = jnp.where(lax.broadcasted_iota(jnp.int32, mixer.shape, 1) < RANK, high.astype(F32), pltpu.roll(low_part.astype(F32), RANK, 1))
+        mix[...] = both.astype(BF16)
 
         whole("vg", it).wait_recv()
         for b in range(nf):
             right = vt_full[it, b]
-            w = mm(mix[0, :, :RANK], right, NN) + mm(mix[1, :, :RANK], right, NN)
+            w = mm(mix[...], jnp.concatenate([right, right], axis=0), NN)
             w_buf[:, b * vb : (b + 1) * vb] = w.astype(BF16)
         whole("fg", it).wait_recv()
 
@@ -345,7 +349,8 @@
                 pltpu.VMEM((ITERS, nf - 1, HALF, LANES), F32),
                 pltpu.VMEM((ITERS, HALF, LANES), F32),
                 pltpu.VMEM((ITERS, nv - 1, HALF, LANES), F32),
-                pltpu.VMEM((2, RANK, LANES), BF16),
+                pltpu.VMEM((RANK, LANES), BF16),
+                pltpu.VMEM((RANK // SUB, SUB, SUB, LANES), F32),
                 dma((nv // fc,)),
                 dma((2,)),
             ]

time: 50.4 us -> 48.6 us (0.964)
  Pallas kernels: 49.5 us -> 47.9 us
    pallas_call x1, Pallas kernels: 43 us -> 41.4 us  [on_device(): pl.pallas_call(functools.partial(sketch_kernel, nv, nf, 4, 2, fc, vc), ou...]
where the time goes in v4:
time: 48.6 us; the launch traced here: 48.5 us
  Pallas kernels  47.9 us (99%)
  between operations  0.64 us (1%)
    pallas_call x1, Pallas kernels, on_device(): pl.pallas_call(functools.partial(sketch_kernel, nv, nf, 4, 2, fc, vc), ou...  41.4 us
    pallas_call x1, Pallas kernels, on_device(): pl.pallas_call(functools.partial(output_kernel, per), out_shape=(jax.Shap...  6.46 us

profile of v4, /device:TPU:0, one launch (start us, length us, event | category | flops | bytes accessed | tf_op | source)
XLA Modules:
  0.0 48.5 jit_solution(2555833342823973049)
XLA Ops:
  0.6 41.4 %sketches.1 = (bf16[2048,2048]{1,0:T(8,128)(2,1)S(1)}, bf16[16,64,128]{2,1,0:T(8,128)(2,1)S(1)}, bf16[64,2048]{1,0:T(8,128)(2,1)S(1)}) custom-call(bf16[2048,2048]{1,0:T(8,128)(2,1)} %m_hbm.1, bf16[64,2048]{1,0:T(8,128)(2,1)} %bitcast.2, bf16[64,2048]{1,0:T(8,128)(2,1)} %bitcast.3), custom_call_target="tpu_custom_call" | custom-call | tf_op jit(solution)/shard_map/sketches/pallas_call | solution.py:328
  42.0 6.5 %outputs.1 = (bf16[2048,2048]{1,0:T(8,128)(2,1)}, bf16[2048,2048]{1,0:T(8,128)(2,1)}) custom-call(bf16[2048,2048]{1,0:T(8,128)(2,1)S(1)} %get-tuple-element.5.m_ref, bf16[16,64,128]{2,1,0:T(8,128)(2,1)S(1)} %get-tuple-element.6.ft_ref, bf16[64,2048]{1,0:T(8,128)(2,1)S(1)} %get-tuple-element.7.w_ref), custom_call_target="tpu_custom_call" | custom-call | tf_op jit(solution)/shard_map/outputs/pallas_call | solution.py:368

commit v5 on v4

--- a/solution.py
+++ b/solution.py
@@ -104,7 +104,7 @@
 
 
 def sketch_kernel(
-    nv, nf, side, cores, fc, vc,
+    nv, nf, side, cores, fc_first, vc,
     m_hbm, vp_hbm, fp_hbm, m_buf, ft_out, w_buf,
     c_buf, vpt, fpt, f_send, f_recv, ft_full, v_send, v_recv, vt_full, t_acc, t_mine, t_recv, t_sum, t_wide, mix, keep,
     m_sem, p_sem, f_sem, fg_sem, v_sem, vg_sem, ta_sem, tb_sem,
@@ -112,13 +112,14 @@
     mv, mf = lax.axis_index("vox"), lax.axis_index("frm")
     frames, voxels = m_buf.shape
     fb, vb = frames // nv, voxels // nf
-    rows, columns = fb * fc, vb * vc
-    row_chunks, column_chunks = nv // fc, nf // vc
-
-    def row_chunk(s):
-        return lax.rem(mv // fc + 1 + s, row_chunks)
-
-    def rows_of(c):
+    fc = fc_first
+    columns, column_chunks = vb * vc, nf // vc
+    rows, row_chunks = fb * fc, nv // fc
+
+    def row_chunk(s, fc=fc):
+        return lax.rem(mv // fc + 1 + s, nv // fc)
+
+    def rows_of(c, rows=rows):
         return pl.ds(pl.multiple_of(c * rows, rows), rows)
 
     def load(s):
@@ -176,24 +177,26 @@
         return to("vox", t_wide.at[it], t_wide.at[it], tb_sem, it, vox_peer(1))
 
     for it in range(ITERS):
+        fc = nv if it else fc_first
+        rows, row_chunks = fb * fc, nv // fc
         src = m_buf if it == 0 else c_buf
 
         def frame_step(s, carry):
-            c = row_chunk(s)
+            c = row_chunk(s, fc)
             if it == 0:
                 load(s).wait()
             else:
                 left = jnp.concatenate([ft_full[it - 1, fc * c + i] for i in range(fc)], axis=1).T
                 for j in range(voxels // WIDE):
-                    at = (rows_of(c), pl.ds(j * WIDE, WIDE))
+                    at = (rows_of(c, rows), pl.ds(j * WIDE, WIDE))
                     low = mm(left, w_buf[:, at[1]], NN)
                     floor, roof = (low - cutoff).astype(BF16), (low + cutoff).astype(BF16)
                     c_buf[at] = jnp.minimum(jnp.maximum(m_buf[at], floor), roof)
-            ft = mm(vpt[...], src[rows_of(c), :], NT)
+            ft = mm(vpt[...], src[rows_of(c, rows), :], NT)
             high, low_part = split(ft)
             for i in range(fc):
                 f_send[it, fc * c + i] = high[:, i * fb : (i + 1) * fb]
-            probe = fpt[:, rows_of(c)]
+            probe = fpt[:, rows_of(c, rows)]
             t_acc[...] += mm(high, probe, NT) + mm(low_part, probe, NT)
             if it > 0:
                 for i in range(fc):

time: 48.6 us -> 48.4 us (level)
  no operation moved by 1% of the time
where the time goes in v5:
time: 48.4 us; the launch traced here: 48.3 us
  Pallas kernels  47.5 us (98%)
  between operations  0.8 us (2%)
    pallas_call x1, Pallas kernels, on_device(): pl.pallas_call(functools.partial(sketch_kernel, nv, nf, 4, 2, fc, vc), ou...  41 us
    pallas_call x1, Pallas kernels, on_device(): pl.pallas_call(functools.partial(output_kernel, per), out_shape=(jax.Shap...  6.46 us

profile of v5, /device:TPU:0, one launch (start us, length us, event | category | flops | bytes accessed | tf_op | source)
XLA Modules:
  0.0 48.3 jit_solution(7743031205487362379)
XLA Ops:
  0.6 41.0 %sketches.1 = (bf16[2048,2048]{1,0:T(8,128)(2,1)S(1)}, bf16[16,64,128]{2,1,0:T(8,128)(2,1)S(1)}, bf16[64,2048]{1,0:T(8,128)(2,1)S(1)}) custom-call(bf16[2048,2048]{1,0:T(8,128)(2,1)} %m_hbm.1, bf16[64,2048]{1,0:T(8,128)(2,1)} %bitcast.2, bf16[64,2048]{1,0:T(8,128)(2,1)} %bitcast.3), custom_call_target="tpu_custom_call" | custom-call | tf_op jit(solution)/shard_map/sketches/pallas_call | solution.py:331
  41.6 6.5 %outputs.1 = (bf16[2048,2048]{1,0:T(8,128)(2,1)}, bf16[2048,2048]{1,0:T(8,128)(2,1)}) custom-call(bf16[2048,2048]{1,0:T(8,128)(2,1)S(1)} %get-tuple-element.5.m_ref, bf16[16,64,128]{2,1,0:T(8,128)(2,1)S(1)} %get-tuple-element.6.ft_ref, bf16[64,2048]{1,0:T(8,128)(2,1)S(1)} %get-tuple-element.7.w_ref), custom_call_target="tpu_custom_call" | custom-call | tf_op jit(solution)/shard_map/outputs/pallas_call | solution.py:371
